TPU v7x, 256 devices: a whole 4x4x8 slice. The times are simulated.
256 devices in a mesh: dp: 16 (over y, x), tensor: 8 (over z), layers: 2 (over core).
Axes of the slice: x: 4, y: 4, z: 8, core: 2. Of those that a mesh axis runs over, the one named last changes fastest.
Arguments:
- section_input: bfloat16 [2, 2048, 4096], P('layers', 'dp', 'tensor'), may hold values from -24 to 24
- out_cotangent: bfloat16 [2048, 4096], P('dp', 'tensor'), may hold values from -24 to 24
- lift_weight: bfloat16 [2, 2048, 4096], P('layers', None, 'tensor'), may hold values from -0.125 to 0.125
- proj_weight: bfloat16 [2, 4096, 4096], P('layers', None, 'tensor'), may hold values from -0.09375 to 0.09375
- lift_mask: int32 [2, 16, 32], P('layers', None, 'tensor'), may hold values 0 or 1
- proj_mask: int32 [2, 32, 32], P('layers', None, 'tensor'), may hold values 0 or 1
- channel_perm: int32 [2, 4096], P('layers'), may hold values from 0 to 4095, each once within a row
- lift_moment: float32 [2, 2048, 4096], P('layers', 'dp', 'tensor'), may hold values from -3 to 3
- lift_square: float32 [2, 2048, 4096], P('layers', 'dp', 'tensor'), may hold values from 0.25 to 1
- proj_moment: float32 [2, 4096, 4096], P('layers', 'dp', 'tensor'), may hold values from -3 to 3
- proj_square: float32 [2, 4096, 4096], P('layers', 'dp', 'tensor'), may hold values from 0.25 to 1
Outputs:
- input_grad: float32 [2, 2048, 4096], P('layers', 'dp', 'tensor')
- log_det: float32 [2], P('layers')
- lift_first: float32 [2, 2048, 4096], P('layers', 'dp', 'tensor')
- lift_second: float32 [2, 2048, 4096], P('layers', 'dp', 'tensor')
- lift_update: float32 [2, 2048, 4096], P('layers', 'dp', 'tensor')
- proj_first: float32 [2, 4096, 4096], P('layers', 'dp', 'tensor')
- proj_second: float32 [2, 4096, 4096], P('layers', 'dp', 'tensor')
- proj_update: float32 [2, 4096, 4096], P('layers', 'dp', 'tensor')
Inputs may be any that keep to these rules, and one draw needn't show every extreme that they name: `channel_perm`: each row orders all 4096 features once. `lift_mask`: 1 keeps a block of 128 x 128 weights, 0 prunes it. `proj_mask`: 1 keeps a block of 128 x 128 weights, 0 prunes it.
All inputs are finite; a program needn't handle non-finite values.
Results may differ from a plain program's by a relative error of at most 0.008.
Values may be sent and summed in bfloat16 or wider, within the bound.
A program may use at most 128 MiB of HBM per device.

v0:
```python
import functools
import jax
import jax.numpy as jnp
from jax import lax
from jax.sharding import Mesh
from jax.sharding import PartitionSpec as P

BLK = 128
ADAM_STEP = 10
CLIP = 4096
DP = ("dp_0", "dp_1")
DP_TENSOR_LAYERS = ("dp_0", "dp_1", "tensor", "layers")
beta_one = 0.9
beta_two = 0.99
adam_eps = 1e-08


def side_by_side(arrays, axis, dim, along):
    both = jnp.concatenate(arrays, axis=along)
    whole, at, finished = (lax.all_gather(both, axis, axis=dim, tiled=True), 0, [])
    for a in arrays:
        finished.append(lax.slice_in_dim(whole, at, at + a.shape[along], axis=along))
        at += a.shape[along]
    return tuple(finished)


def over_pieces(array, axis):
    return lax.all_gather(array, axis).astype(jnp.float32).sum(0)


def passed_along(block, axis, distance):
    devices = range(lax.axis_size(axis))
    route = [(i - distance, i) for i in devices if i - distance in devices]
    return lax.ppermute(block, axis, route)


def over_axes(array, axes):
    return functools.reduce(lax.psum, axes, array)


def expand_blocks(block_mask):
    blk_rows, blk_cols = block_mask.shape
    widened = jnp.broadcast_to((block_mask > 0)[:, None, :, None], (blk_rows, BLK, blk_cols, BLK))
    return widened.reshape(blk_rows * BLK, blk_cols * BLK)


def contract_rows(left_mat, right_mat):
    return lax.dot_general(
        left_mat, right_mat, (((0,), (0,)), ((), ())), preferred_element_type=jnp.float32
    )


def contract_cols(left_mat, right_mat):
    return lax.dot_general(
        left_mat, right_mat, (((1,), (1,)), ((), ())), preferred_element_type=jnp.float32
    )


def adam_step(gradient, kept, moment, square, factor):
    scaled = gradient * factor
    new_first = jnp.where(kept, beta_one * moment + (1.0 - beta_one) * scaled, moment)
    new_second = jnp.where(kept, beta_two * square + (1.0 - beta_two) * scaled * scaled, square)
    bias_one = 1.0 - beta_one**ADAM_STEP
    bias_two = 1.0 - beta_two**ADAM_STEP
    update = jnp.where(
        kept, new_first / bias_one / (jnp.sqrt(new_second / bias_two) + adam_eps), 0.0
    )
    return (new_first[None], new_second[None], update[None])


def per_device(
    section_input,
    out_cotangent,
    lift_weight,
    proj_weight,
    lift_mask,
    proj_mask,
    channel_perm,
    lift_moment,
    lift_square,
    proj_moment,
    proj_square,
):
    section_idx = lax.axis_index("layers")
    dp_size = lax.axis_size(DP)
    dp_index = lax.axis_index(DP)
    tensor_size = lax.axis_size("tensor")
    tensor_index = lax.axis_index("tensor")
    tokens, gathered_cot = side_by_side((section_input[0], out_cotangent), "tensor", 1, 0)
    channel_order = channel_perm[0]
    feat_width = channel_order.shape[0]
    half_width = feat_width // 2
    tok_rows = tokens.shape[0]
    lift_keep = expand_blocks(lift_mask[0])
    proj_keep = expand_blocks(proj_mask[0])
    lift_eff = jnp.where(lift_keep, lift_weight[0], jnp.zeros((), jnp.bfloat16))
    proj_eff = jnp.where(proj_keep, proj_weight[0], jnp.zeros((), jnp.bfloat16))
    permuted = jnp.take(tokens, channel_order, axis=1)
    cond_side = permuted[:, :half_width]
    moved_side = permuted[:, half_width:].astype(jnp.float32)
    pre_act = jnp.dot(cond_side, lift_eff, preferred_element_type=jnp.float32)
    hidden = jax.nn.silu(pre_act).astype(jnp.bfloat16)
    shared = lax.psum(contract_cols(hidden, proj_eff).astype(jnp.bfloat16), "tensor").astype(
        jnp.float32
    )
    raw_scale = shared[:, :half_width]
    shift_term = shared[:, half_width:]
    scale_term = jax.nn.sigmoid(raw_scale + 2.0)
    keep_part = 1.0 - scale_term
    squash = jax.nn.sigmoid(pre_act)
    silu_slope = squash * (1.0 + pre_act * (1.0 - squash))
    inverse = (
        jnp.zeros((feat_width,), jnp.int32)
        .at[channel_order]
        .set(jnp.arange(feat_width, dtype=jnp.int32))
    )
    own_cols = half_width // tensor_size
    own_raw = lax.dynamic_slice_in_dim(raw_scale, tensor_index * own_cols, own_cols, 1)
    log_part = jnp.sum(jax.nn.log_sigmoid(own_raw + 2.0))

    def backward(grad_out):
        grad_cond = grad_out[:, :half_width]
        grad_moved = grad_out[:, half_width:]
        grad_raw = grad_moved * (moved_side + shift_term) * scale_term * keep_part - keep_part
        grad_shift = grad_moved * scale_term
        grad_st = jnp.concatenate([grad_raw, grad_shift], axis=1).astype(jnp.bfloat16)
        grad_act = jnp.dot(grad_st, proj_eff, preferred_element_type=jnp.float32)
        grad_pre = (grad_act * silu_slope).astype(jnp.bfloat16)
        grad_inputs = grad_cond + over_pieces(
            contract_cols(grad_pre, lift_eff).astype(jnp.bfloat16), "tensor"
        ).astype(jnp.float32)
        grad_mixed = jnp.concatenate([grad_inputs, grad_shift], axis=1)
        return (grad_mixed, grad_st, grad_pre)

    incoming = gathered_cot.astype(jnp.float32)
    early_mixed = backward(incoming)[0]
    early_grad = jnp.take(early_mixed, inverse, axis=1)
    passed = passed_along(early_grad.astype(jnp.bfloat16), "layers", -1)
    arriving = jnp.where(section_idx == 0, passed.astype(jnp.float32), incoming)
    grad_mixed, grad_st, grad_pre = backward(arriving)
    lift_rows = lift_moment.shape[1]
    proj_rows = proj_moment.shape[1]
    cond_cols, st_cols = (
        lax.all_to_all(cond_side, DP, split_axis=1, concat_axis=0, tiled=True),
        lax.all_to_all(grad_st, DP, split_axis=1, concat_axis=0, tiled=True),
    )
    pieces = side_by_side((grad_pre, hidden), DP, 0, 1)
    lift_grad = contract_rows(cond_cols, pieces[0])
    proj_grad = contract_rows(st_cols, pieces[1])
    lift_own = lax.dynamic_slice_in_dim(lift_keep, dp_index * lift_rows, lift_rows, 0)
    proj_own = lax.dynamic_slice_in_dim(proj_keep, dp_index * proj_rows, proj_rows, 0)
    lift_grad = jnp.where(lift_own, lift_grad, 0.0)
    proj_grad = jnp.where(proj_own, proj_grad, 0.0)
    local_sq = jnp.sum(lift_grad * lift_grad) + jnp.sum(proj_grad * proj_grad)
    section_slots = jnp.where(jnp.arange(2) == section_idx, log_part, 0.0)
    log_slots, square_total = (
        over_axes(section_slots, DP_TENSOR_LAYERS),
        over_axes(local_sq, DP_TENSOR_LAYERS),
    )
    log_total = jnp.sum(jnp.where(jnp.arange(2) == section_idx, log_slots, 0.0))
    factor = jnp.minimum(1.0, CLIP / (jnp.sqrt(square_total) + 1e-06))
    lift_out = adam_step(lift_grad, lift_own, lift_moment[0], lift_square[0], factor)
    proj_out = adam_step(proj_grad, proj_own, proj_moment[0], proj_square[0], factor)
    grad_cols = feat_width // tensor_size
    own_inverse = lax.dynamic_slice_in_dim(inverse, tensor_index * grad_cols, grad_cols, 0)
    input_grad = jnp.take(grad_mixed, own_inverse, axis=1)[None]
    log_det = (log_total / (tok_rows * dp_size * half_width)).reshape(1)
    return (
        input_grad,
        log_det,
        lift_out[0],
        lift_out[1],
        lift_out[2],
        proj_out[0],
        proj_out[1],
        proj_out[2],
    )


def solution(mesh):
    finer = Mesh(
        mesh.devices.reshape(4, 4, mesh.shape["tensor"], mesh.shape["layers"]),
        ("dp_0", "dp_1", "tensor", "layers"),
    )
    return jax.shard_map(
        per_device,
        mesh=finer,
        in_specs=(
            P("layers", DP, "tensor"),
            P(DP, "tensor"),
            P("layers", None, "tensor"),
            P("layers", None, "tensor"),
            P("layers", None, "tensor"),
            P("layers", None, "tensor"),
            P("layers", None),
            P("layers", DP, "tensor"),
            P("layers", DP, "tensor"),
            P("layers", DP, "tensor"),
            P("layers", DP, "tensor"),
        ),
        out_specs=(
            P("layers", DP, "tensor"),
            P("layers"),
            P("layers", DP, "tensor"),
            P("layers", DP, "tensor"),
            P("layers", DP, "tensor"),
            P("layers", DP, "tensor"),
            P("layers", DP, "tensor"),
            P("layers", DP, "tensor"),
        ),
        check_vma=False,
    )
```

profile of v0, /device:TPU:1, one launch (start us, length us, event | category | flops | bytes accessed | tf_op | source)
XLA Modules:
  0.0 439.0 jit_solution(12635905943048459885)
XLA Ops:
  7.2 1.7 pad_maximum_fusion.3
  12.0 38.8 %all-gather.7.cloned.1.call-done = bf16[256,4096]{1,0:T(8,128)(2,1)} async-done(((bf16[256,512]{1,0:T(8,128)(2,1)}), bf16[256,4096]{1,0:T(8,128)(2,1)}) %all-gather.7.cloned.1.call-update) | async-done | bytes 2097168 | tf_op jit(solution)/shard_map/all_gather | solution.py:20
  50.8 3.2 slice_convert_fusion
  54.7 12.1 %gather_fusion = bf16[4096,128]{1,0:T(8,128)(2,1)S(1)} fusion(bf16[128,4096]{0,1:T(8,128)(2,1)S(1)} %copy.27, s32[4096]{0:T(1024)S(1)} %broadcast_clamp_fusion), kind=kCustom, calls=%fused_computation | custom fusion | bytes 2113536 | tf_op jit(solution)/shard_map/jit(_take)/gather | solution.py:98
  73.8 2.8 convolution_convert_fusion
  76.7 74.5 %all-reduce.6.cloned.1.call-done = bf16[128,4096]{1,0:T(8,128)(2,1)} async-done(((bf16[128,4096]{1,0:T(8,128)(2,1)}), bf16[128,4096]{1,0:T(8,128)(2,1)}) %all-reduce.6.cloned.1.call-update) | async-done | bytes 1048592 | tf_op jit(solution)/shard_map/psum | solution.py:103
  152.6 2.6 fusion.12
  156.4 6.9 %convolution_convert_fusion.2 = bf16[128,2048]{1,0:T(8,128)(2,1)} fusion(bf16[1,4096,512]{2,1,0:T(8,128)(2,1)} %param.14, bf16[128,2048]{1,0:T(8,128)(2,1)} %slice_multiply_fusion.1, bf16[128,2048]{1,0:T(8,128)(2,1)} %fusion.12, bf16[1,2048,512]{2,1,0:T(8,128)(2,1)} %param.13, f32[128,512]{1,0:T(8,128)} %get-tuple-element.46, ...), kind=kOutput, calls=%fused_computation.11 | convolution fusion | flops 811401216 | bytes 11272192 | tf_op jit(solution)/shard_map/dot_general | solution.py:54
  163.4 15.5 %scatter_custom_fusion = s32[4096]{0:T(1024)S(1)} fusion(s32[4096]{0:T(1024)S(1)} %bitcast.161, s32[4096]{0:T(1024)S(1)} %iota.7, s32[]{:T(128)} %constant.33.clone.1), kind=kCustom, calls=%fused_computation.87 | custom fusion | bytes 16388 | tf_op jit(solution)/shard_map/scatter | solution.py:115
  179.0 41.9 %all-gather.11.cloned.1.call-done = bf16[1024,2048]{1,0:T(8,128)(2,1)} async-done(((bf16[128,2048]{1,0:T(8,128)(2,1)}), bf16[1024,2048]{1,0:T(8,128)(2,1)}) %all-gather.11.cloned.1.call-update) | async-done | bytes 4194320 | tf_op jit(solution)/shard_map/all_gather | solution.py:28
  220.9 3.1 convert_reduce_fusion.1
  226.2 1.6 copy.31
  227.9 15.0 %gather_fusion.1 = bf16[4096,128]{1,0:T(8,128)(2,1)} fusion(bf16[128,4096]{0,1:T(8,128)(2,1)S(1)} %copy.31, s32[4096]{0:T(1024)S(1)} %fusion.33), kind=kCustom, calls=%fused_computation.1 | custom fusion | bytes 2113536 | tf_op jit(solution)/shard_map/jit(_take)/gather | solution.py:137
  245.5 3.7 collective-permute-start
  250.9 1.9 convert_select_fusion
  258.0 1.7 convolution_convert_fusion.1
  260.5 2.4 copy.69
  268.1 6.5 %all-to-all-start.1 = ((bf16[128,16,256]{2,0,1:T(8,128)(2,1)}), bf16[128,16,256]{2,0,1:T(8,128)(2,1)S(1)}, u32[]{:S(2)}, u32[]{:S(2)}) async-start(bf16[128,16,256]{2,0,1:T(8,128)(2,1)} %pad_maximum_fusion.2), calls=%async_computation.1 | async-start | bytes 2097152 | tf_op jit(solution)/shard_map/all_to_all | solution.py:145
  274.7 38.1 %all-gather.13.cloned.1.call-done = bf16[1024,2048]{1,0:T(8,128)(2,1)} async-done(((bf16[128,2048]{1,0:T(8,128)(2,1)}), bf16[1024,2048]{1,0:T(8,128)(2,1)}) %all-gather.13.cloned.1.call-update) | async-done | bytes 4194320 | tf_op jit(solution)/shard_map/all_gather | solution.py:28
  312.8 3.1 convert_reduce_fusion
  317.3 1.8 copy.33
  319.1 2.6 gather_fusion.2
  321.8 6.5 %all-to-all-start = ((bf16[128,16,128]{2,0,1:T(8,128)(2,1)}), bf16[128,16,128]{2,0,1:T(8,128)(2,1)S(1)}, u32[]{:S(2)}, u32[]{:S(2)}) async-start(bf16[128,16,128]{2,0,1:T(8,128)(2,1)} %copy_bitcast_fusion.4), calls=%async_computation | async-start | bytes 1048576 | tf_op jit(solution)/shard_map/all_to_all | solution.py:144
  328.5 46.1 %all-gather.9.cloned.1.call-done = bf16[2048,1024]{1,0:T(8,128)(2,1)} async-done(((bf16[128,1024]{1,0:T(8,128)(2,1)}), bf16[2048,1024]{1,0:T(8,128)(2,1)}) %all-gather.9.cloned.1.call-update) | async-done | bytes 4194320 | tf_op jit(solution)/shard_map/all_gather | solution.py:20
  374.6 3.7 multiply_reduce_fusion
  378.3 2.8 multiply_reduce_fusion.1
  383.4 8.9 %all-reduce.2 = (f32[2]{0:T(128)S(1)}, f32[]{:T(128)}) all-reduce(f32[2]{0:T(128)S(1)} %compare_select_fusion.6, f32[]{:T(128)S(6)} %add.161), channel_id=1, replica_groups=mesh['dp_0'=4,'dp_1'=4,'tensor'=8,'layers'=2] {'dp_0'}, use_global_device_ids=true, to_apply=%region_5.6 | all-reduce | flops 3 | bytes 24 | tf_op jit(solution)/shard_map/psum | solution.py:38
  392.3 7.2 %all-reduce.1 = (f32[2]{0:T(128)S(1)}, f32[]{:T(128)}) all-reduce(f32[2]{0:T(128)S(1)} %get-tuple-element.28, f32[]{:T(128)} %get-tuple-element.29), channel_id=1, replica_groups=mesh['dp_0'=4,'dp_1'=4,'tensor'=8,'layers'=2] {'dp_1'}, use_global_device_ids=true, to_apply=%region_6.7 | all-reduce | flops 3 | bytes 24 | tf_op jit(solution)/shard_map/psum | solution.py:38
  399.5 14.3 %all-reduce = (f32[2]{0:T(128)S(1)}, f32[]{:T(128)}) all-reduce(f32[2]{0:T(128)S(1)} %get-tuple-element.26, f32[]{:T(128)} %get-tuple-element.27), channel_id=1, replica_groups=mesh['dp_0'=4,'dp_1'=4,'tensor'=8,'layers'=2] {'tensor'}, use_global_device_ids=true, to_apply=%region_7.8 | all-reduce | flops 3 | bytes 24 | tf_op jit(solution)/shard_map/psum | solution.py:38
  413.8 11.3 %all-reduce.3 = (f32[2]{0:T(128)S(1)}, f32[]{:T(128)}) all-reduce(f32[2]{0:T(128)S(1)} %get-tuple-element.24, f32[]{:T(128)} %get-tuple-element.25), channel_id=1, replica_groups=mesh['dp_0'=4,'dp_1'=4,'tensor'=8,'layers'=2] {'layers'}, use_global_device_ids=true, to_apply=%region_8.9 | all-reduce | flops 3 | bytes 24 | tf_op jit(solution)/shard_map/psum | solution.py:38
  427.1 2.4 select_bitcast_fusion.1
  429.5 1.9 select_bitcast_fusion.2
  (112 shorter events, 33.2 us)
Async XLA Ops:
  7.2 43.7 %all-gather.7.cloned.1.call-start = ((), (), s32[]{:S(2)}) async-start(), calls=%async_computation.2 | async-start | bytes 2359296 | tf_op jit(solution)/shard_map/all_gather | solution.py:20
  8.9 142.2 %all-reduce.6.cloned.1.call-start = ((), (), s32[]{:S(2)}) async-start(), calls=%async_computation.3 | async-start | bytes 2097152 | tf_op jit(solution)/shard_map/psum | solution.py:103
  67.4 2.4 copy-start.27
  67.6 85.0 %copy-start.7 = (bf16[128,4096]{1,0:T(8,128)(2,1)}, bf16[128,4096]{1,0:T(8,128)(2,1)S(1)}, u32[]{:S(2)}) copy-start(bf16[128,4096]{1,0:T(8,128)(2,1)S(1)} %select_bitcast_fusion) | copy-start | bytes 3145732
  68.2 3.1 copy-start.10
  69.8 4.1 copy-start.25
  76.6 144.3 %all-gather.11.cloned.1.call-start = ((), (), s32[]{:S(2)}) async-start(), calls=%async_computation.5 | async-start | bytes 4718592 | tf_op jit(solution)/shard_map/all_gather | solution.py:28
  152.6 2.6 copy-start
  163.4 149.4 %all-gather.13.cloned.1.call-start = ((), (), s32[]{:S(2)}) async-start(), calls=%async_computation.6 | async-start | bytes 4718592 | tf_op jit(solution)/shard_map/all_gather | solution.py:28
  220.9 3.1 copy-start.1
  245.5 5.4 %collective-permute-start = (bf16[128,4096]{1,0:T(8,128)(2,1)}, bf16[128,4096]{1,0:T(8,128)(2,1)}, u32[]{:S(2)}, u32[]{:S(2)}) collective-permute-start(bf16[128,4096]{1,0:T(8,128)(2,1)} %fusion.14), channel_id=1, source_target_pairs={{1,0},{3,2},{5,4},{7,6},{9,8},{11,10},{13,12},{15,14},{17,16},{19,... | collective-permute-start | bytes 3145736 | tf_op jit(solution)/shard_map/ppermute | solution.py:34
  249.3 3.6 copy-start.8
  250.9 3.7 copy-start.26
  252.9 3.0 copy-start.5
  252.9 3.2 copy-start.29
  254.5 2.9 copy-start.16
  254.5 2.9 copy-start.18
  256.0 1.9 copy-start.28
  258.0 2.6 copy-start.6
  259.7 114.9 %all-gather.9.cloned.1.call-start = ((), (), s32[]{:S(2)}) async-start(), calls=%async_computation.4 | async-start | bytes 4456448 | tf_op jit(solution)/shard_map/all_gather | solution.py:20
  260.5 2.4 copy-start.13
  262.9 2.5 copy-start.9
  264.5 2.5 copy-start.17
  264.5 2.5 copy-start.19
  268.1 53.6 %all-to-all-start.1 = ((bf16[128,16,256]{2,0,1:T(8,128)(2,1)}), bf16[128,16,256]{2,0,1:T(8,128)(2,1)S(1)}, u32[]{:S(2)}, u32[]{:S(2)}) async-start(bf16[128,16,256]{2,0,1:T(8,128)(2,1)} %pad_maximum_fusion.2), calls=%async_computation.1 | async-start | bytes 2097152 | tf_op jit(solution)/shard_map/all_to_all | solution.py:145
  312.8 3.1 copy-start.3
  321.8 56.6 %all-to-all-start = ((bf16[128,16,128]{2,0,1:T(8,128)(2,1)}), bf16[128,16,128]{2,0,1:T(8,128)(2,1)S(1)}, u32[]{:S(2)}, u32[]{:S(2)}) async-start(bf16[128,16,128]{2,0,1:T(8,128)(2,1)} %copy_bitcast_fusion.4), calls=%async_computation | async-start | bytes 1048576 | tf_op jit(solution)/shard_map/all_to_all | solution.py:144
  378.3 48.8 %copy-start.20 = (f32[1,256,512]{2,1,0:T(8,128)S(1)}, f32[1,256,512]{2,1,0:T(8,128)}, u32[]{:S(2)}) copy-start(f32[1,256,512]{2,1,0:T(8,128)} %param.20) | copy-start | bytes 1572868
  378.3 48.8 %copy-start.21 = (f32[1,256,512]{2,1,0:T(8,128)S(1)}, f32[1,256,512]{2,1,0:T(8,128)}, u32[]{:S(2)}) copy-start(f32[1,256,512]{2,1,0:T(8,128)} %param.21) | copy-start | bytes 1572868
  378.3 48.8 %copy-start.22 = (f32[256,512]{1,0:T(8,128)S(1)}, f32[256,512]{1,0:T(8,128)}, u32[]{:S(2)}) copy-start(f32[256,512]{1,0:T(8,128)} %get-tuple-element.50) | copy-start | bytes 1572868
  381.2 48.3 %copy-start.23 = (f32[1,128,512]{2,1,0:T(8,128)S(1)}, f32[1,128,512]{2,1,0:T(8,128)}, u32[]{:S(2)}) copy-start(f32[1,128,512]{2,1,0:T(8,128)} %param.18) | copy-start | bytes 786436
  381.2 48.3 %copy-start.24 = (f32[1,128,512]{2,1,0:T(8,128)S(1)}, f32[1,128,512]{2,1,0:T(8,128)}, u32[]{:S(2)}) copy-start(f32[1,128,512]{2,1,0:T(8,128)} %param.19) | copy-start | bytes 786436
  (6 other events, 8.1 us)
Sparse Core Ops, SparseCore 0:
  10.3 40.4 all-gather.6
  76.7 74.3 all-reduce.5
  163.5 57.4 all-gather.10
  259.8 52.8 all-gather.12
  315.6 58.9 all-gather.8
where the time goes:
time: 440 us; the launch traced here: 439 us
  waiting for transfers between devices  241 us (55%)
  local copies, waits for them, and re-layouts  66.6 us (15%)
  blocking collectives  41.7 us (9%)
  other arithmetic  32.9 us (7%)
  matrix products  20.9 us (5%)
  between operations  18.8 us (4%)
  starting transfers between devices  17 us (4%)
    all_gather x2, waiting for transfers between devices, side_by_side(): lax.all_gather(both, axis, axis=dim, tiled=True)  84.9 us
    all_gather x2, waiting for transfers between devices, over_pieces(): return lax.all_gather(array, axis).astype(jnp.float32).sum(0)  80 us
    psum x1, waiting for transfers between devices, per_device(): lax.psum(contract_cols(hidden, proj_eff).astype(jnp.bfloat16), 'tensor')  74.5 us
    psum x4, blocking collectives, over_axes(): return functools.reduce(lax.psum, axes, array)  41.7 us
    gather x2, local copies, waits for them, and re-layouts, per_device(): early_grad = jnp.take(early_mixed, inverse, axis=1)  16.5 us
    scatter x1, local copies, waits for them, and re-layouts, per_device(): inverse = jnp.zeros((feat_width,), jnp.int32).at[channel_order].set(jnp.a...  15.5 us
    gather x2, local copies, waits for them, and re-layouts, per_device(): permuted = jnp.take(tokens, channel_order, axis=1)  12.7 us
    unnamed x63, local copies, waits for them, and re-layouts  12.1 us
  transfers between devices with their start and end apart: 8, of which 6 were waited for; matrix products, arithmetic and copies ran while one was open for 9% of the time, Pallas kernels for 0%

commit v1 on v0

--- a/solution.py
+++ b/solution.py
@@ -100,9 +100,9 @@
     moved_side = permuted[:, half_width:].astype(jnp.float32)
     pre_act = jnp.dot(cond_side, lift_eff, preferred_element_type=jnp.float32)
     hidden = jax.nn.silu(pre_act).astype(jnp.bfloat16)
-    shared = lax.psum(contract_cols(hidden, proj_eff).astype(jnp.bfloat16), "tensor").astype(
-        jnp.float32
-    )
+    shared = jnp.sum(
+        lax.all_gather(contract_cols(hidden, proj_eff).astype(jnp.bfloat16), "tensor"), axis=0
+    ).astype(jnp.float32)
     raw_scale = shared[:, :half_width]
     shift_term = shared[:, half_width:]
     scale_term = jax.nn.sigmoid(raw_scale + 2.0)

time: 440 us -> 463 us (1.052)
  waiting for transfers between devices: 241 us -> 258 us
  other arithmetic: 32.9 us -> 40.6 us
    all_gather x0 -> x1, waiting for transfers between devices: none -> 96.8 us  [per_device(): lax.all_gather(contract_cols(hidden, proj_eff).astype(jnp.bfloat16), 'ten...]
    psum x1 -> x0, waiting for transfers between devices: 74.5 us -> none  [per_device(): lax.psum(contract_cols(hidden, proj_eff).astype(jnp.bfloat16), 'tensor')]
    reduce_sum x0 -> x1, other arithmetic: none -> 4.9 us  [per_device(): jnp.sum(lax.all_gather(contract_cols(hidden, proj_eff).astype(jnp.bfloat1...]
    gather x2 -> x1, local copies, waits for them, and re-layouts: 16.5 us -> 15 us  [per_device(): early_grad = jnp.take(early_mixed, inverse, axis=1)]
    gather x2 -> x1, local copies, waits for them, and re-layouts: 12.7 us -> 12.1 us  [per_device(): permuted = jnp.take(tokens, channel_order, axis=1)]
  transfers between devices with their start and end apart: 8 -> 8, of which waited for: 6 -> 6; matrix products, arithmetic and copies ran while one was open for 9% -> 8% of each run, Pallas kernels for 0% -> 0%
where the time goes in v1:
time: 463 us; the launch traced here: 462 us
  waiting for transfers between devices  258 us (56%)
  local copies, waits for them, and re-layouts  64.4 us (14%)
  blocking collectives  41.8 us (9%)
  other arithmetic  40.6 us (9%)
  matrix products  21.2 us (5%)
  between operations  18.8 us (4%)
  starting transfers between devices  17.1 us (4%)
    all_gather x1, waiting for transfers between devices, per_device(): lax.all_gather(contract_cols(hidden, proj_eff).astype(jnp.bfloat16), 'ten...  96.8 us
    all_gather x2, waiting for transfers between devices, side_by_side(): lax.all_gather(both, axis, axis=dim, tiled=True)  83.9 us
    all_gather x2, waiting for transfers between devices, over_pieces(): return lax.all_gather(array, axis).astype(jnp.float32).sum(0)  75.4 us
    psum x4, blocking collectives, over_axes(): return functools.reduce(lax.psum, axes, array)  41.8 us
    scatter x1, local copies, waits for them, and re-layouts, per_device(): inverse = jnp.zeros((feat_width,), jnp.int32).at[channel_order].set(jnp.a...  15.7 us
    gather x1, local copies, waits for them, and re-layouts, per_device(): early_grad = jnp.take(early_mixed, inverse, axis=1)  15 us
    unnamed x63, local copies, waits for them, and re-layouts  13.3 us
    gather x1, local copies, waits for them, and re-layouts, per_device(): permuted = jnp.take(tokens, channel_order, axis=1)  12.1 us
  transfers between devices with their start and end apart: 8, of which 6 were waited for; matrix products, arithmetic and copies ran while one was open for 8% of the time, Pallas kernels for 0%

profile of v1, /device:TPU:1, one launch (start us, length us, event | category | flops | bytes accessed | tf_op | source)
XLA Modules:
  0.0 461.6 jit_solution(13504489489482705431)
XLA Ops:
  13.1 37.7 %all-gather.9.cloned.1.call-done = bf16[256,4096]{0,1:T(8,128)(2,1)} async-done(((bf16[256,512]{0,1:T(8,128)(2,1)}), bf16[256,4096]{0,1:T(8,128)(2,1)}) %all-gather.9.cloned.1.call-update) | async-done | bytes 2097168 | tf_op jit(solution)/shard_map/all_gather | solution.py:20
  50.8 3.2 slice_convert_fusion
  54.0 12.1 %gather_fusion = bf16[4096,128]{1,0:T(8,128)(2,1)S(1)} fusion(bf16[128,4096]{0,1:T(8,128)(2,1)S(1)} %get-tuple-element.49, s32[4096]{0:T(1024)S(1)} %broadcast_clamp_fusion), kind=kCustom, calls=%fused_computation | custom fusion | bytes 2113536 | tf_op jit(solution)/shard_map/jit(_take)/gather | solution.py:98
  66.1 2.1 select_bitcast_fusion
  73.0 2.8 convolution_convert_fusion
  75.9 96.8 %all-gather.13.cloned.1.call-done = bf16[1024,4096]{1,0:T(8,128)(2,1)} async-done(((bf16[128,4096]{1,0:T(8,128)(2,1)}), bf16[1024,4096]{1,0:T(8,128)(2,1)}) %all-gather.13.cloned.1.call-update) | async-done | bytes 8388624 | tf_op jit(solution)/shard_map/all_gather | solution.py:104
  172.6 4.9 %reduce_sum.66 = bf16[128,4096]{1,0:T(8,128)(2,1)S(1)} reduce(bf16[8,128,4096]{2,1,0:T(8,128)(2,1)} %bitcast.133, bf16[]{:T(256)} %constant.41.clone.1), dimensions={0}, to_apply=%region_1.2 | reduce | flops 3670016 | bytes 9437186 | tf_op jit(solution)/shard_map/reduce_sum | solution.py:103
  178.4 1.8 copy-done
  182.8 7.4 %convolution_convert_fusion.2 = bf16[128,2048]{1,0:T(8,128)(2,1)} fusion(bf16[1,4096,512]{2,1,0:T(8,128)(2,1)} %param.14, bf16[128,2048]{0,1:T(8,128)(2,1)} %slice_multiply_fusion.1, bf16[128,2048]{0,1:T(8,128)(2,1)} %fusion.12, bf16[1,2048,512]{2,1,0:T(8,128)(2,1)} %param.13, f32[128,512]{1,0:T(8,128)} %get-tuple-element.54, ...), kind=kOutput, calls=%fused_computation.11 | convolution fusion | flops 811401216 | bytes 11272192 | tf_op jit(solution)/shard_map/dot_general | solution.py:54
  190.3 15.7 %scatter_custom_fusion = s32[4096]{0:T(1024)S(1)} fusion(s32[4096]{0:T(1024)S(1)} %bitcast.155, s32[4096]{0:T(1024)S(1)} %iota.7, s32[]{:T(128)} %constant.34.clone.1), kind=kCustom, calls=%fused_computation.82 | custom fusion | bytes 16388 | tf_op jit(solution)/shard_map/scatter | solution.py:115
  206.0 37.7 %all-gather.15.cloned.1.call-done = bf16[1024,2048]{1,0:T(8,128)(2,1)} async-done(((bf16[128,2048]{1,0:T(8,128)(2,1)}), bf16[1024,2048]{1,0:T(8,128)(2,1)}) %all-gather.15.cloned.1.call-update) | async-done | bytes 4194320 | tf_op jit(solution)/shard_map/all_gather | solution.py:28
  243.7 3.0 convert_reduce_fusion.1
  248.1 1.7 slice_add_fusion.2
  249.9 15.0 %gather_fusion.1 = bf16[4096,128]{1,0:T(8,128)(2,1)} fusion(bf16[128,4096]{0,1:T(8,128)(2,1)S(1)} %pad_maximum_fusion, s32[4096]{0:T(1024)S(1)} %fusion.32), kind=kCustom, calls=%fused_computation.1 | custom fusion | bytes 2113536 | tf_op jit(solution)/shard_map/jit(_take)/gather | solution.py:137
  264.9 4.3 fusion.14
  269.2 3.8 collective-permute-start
  274.5 1.9 convert_select_fusion
  281.7 1.7 convolution_convert_fusion.1
  284.2 2.3 copy.68
  292.1 6.6 %all-to-all-start.1 = ((bf16[128,16,256]{2,0,1:T(8,128)(2,1)}), bf16[128,16,256]{2,0,1:T(8,128)(2,1)}, u32[]{:S(2)}, u32[]{:S(2)}) async-start(bf16[128,16,256]{2,0,1:T(8,128)(2,1)} %pad_maximum_fusion.2), calls=%async_computation.1 | async-start | bytes 2097152 | tf_op jit(solution)/shard_map/all_to_all | solution.py:145
  298.7 37.7 %all-gather.17.cloned.1.call-done = bf16[1024,2048]{1,0:T(8,128)(2,1)} async-done(((bf16[128,2048]{1,0:T(8,128)(2,1)}), bf16[1024,2048]{1,0:T(8,128)(2,1)}) %all-gather.17.cloned.1.call-update) | async-done | bytes 4194320 | tf_op jit(solution)/shard_map/all_gather | solution.py:28
  336.4 4.0 convert_reduce_fusion
  344.8 6.5 %all-to-all-start = ((bf16[128,16,128]{2,0,1:T(8,128)(2,1)}), bf16[128,16,128]{2,0,1:T(8,128)(2,1)S(1)}, u32[]{:S(2)}, u32[]{:S(2)}) async-start(bf16[128,16,128]{2,0,1:T(8,128)(2,1)} %copy.39), calls=%async_computation | async-start | bytes 1048576 | tf_op jit(solution)/shard_map/all_to_all | solution.py:144
  351.5 46.2 %all-gather.11.cloned.1.call-done = bf16[2048,1024]{1,0:T(8,128)(2,1)} async-done(((bf16[128,1024]{1,0:T(8,128)(2,1)}), bf16[2048,1024]{1,0:T(8,128)(2,1)}) %all-gather.11.cloned.1.call-update) | async-done | bytes 4194320 | tf_op jit(solution)/shard_map/all_gather | solution.py:20
  397.7 3.3 multiply_reduce_fusion
  401.0 2.8 multiply_reduce_fusion.1
  405.9 8.9 %all-reduce.2 = (f32[2]{0:T(128)S(1)}, f32[]{:T(128)}) all-reduce(f32[2]{0:T(128)S(1)} %compare_select_fusion.6, f32[]{:T(128)S(6)} %add.159), channel_id=1, replica_groups=mesh['dp_0'=4,'dp_1'=4,'tensor'=8,'layers'=2] {'dp_0'}, use_global_device_ids=true, to_apply=%region_5.6 | all-reduce | flops 3 | bytes 24 | tf_op jit(solution)/shard_map/psum | solution.py:38
  414.8 7.2 %all-reduce.1 = (f32[2]{0:T(128)S(1)}, f32[]{:T(128)}) all-reduce(f32[2]{0:T(128)S(1)} %get-tuple-element.36, f32[]{:T(128)} %get-tuple-element.37), channel_id=1, replica_groups=mesh['dp_0'=4,'dp_1'=4,'tensor'=8,'layers'=2] {'dp_1'}, use_global_device_ids=true, to_apply=%region_6.7 | all-reduce | flops 3 | bytes 24 | tf_op jit(solution)/shard_map/psum | solution.py:38
  422.0 14.3 %all-reduce = (f32[2]{0:T(128)S(1)}, f32[]{:T(128)}) all-reduce(f32[2]{0:T(128)S(1)} %get-tuple-element.34, f32[]{:T(128)} %get-tuple-element.35), channel_id=1, replica_groups=mesh['dp_0'=4,'dp_1'=4,'tensor'=8,'layers'=2] {'tensor'}, use_global_device_ids=true, to_apply=%region_7.8 | all-reduce | flops 3 | bytes 24 | tf_op jit(solution)/shard_map/psum | solution.py:38
  436.3 11.3 %all-reduce.3 = (f32[2]{0:T(128)S(1)}, f32[]{:T(128)}) all-reduce(f32[2]{0:T(128)S(1)} %get-tuple-element.32, f32[]{:T(128)} %get-tuple-element.33), channel_id=1, replica_groups=mesh['dp_0'=4,'dp_1'=4,'tensor'=8,'layers'=2] {'layers'}, use_global_device_ids=true, to_apply=%region_8.9 | all-reduce | flops 3 | bytes 24 | tf_op jit(solution)/shard_map/psum | solution.py:38
  449.7 2.4 select_bitcast_fusion.1
  452.1 1.9 select_bitcast_fusion.2
  (114 shorter events, 33.9 us)
Async XLA Ops:
  7.2 43.7 %all-gather.9.cloned.1.call-start = ((), (), s32[]{:S(2)}) async-start(), calls=%async_computation.2 | async-start | bytes 2359296 | tf_op jit(solution)/shard_map/all_gather | solution.py:20
  10.0 162.6 %all-gather.13.cloned.1.call-start = ((), (), s32[]{:S(2)}) async-start(), calls=%async_computation.4 | async-start | bytes 9437184 | tf_op jit(solution)/shard_map/all_gather | solution.py:104
  66.1 2.8 copy-start.26
  68.3 2.3 copy-start.8
  68.9 4.1 copy-start.24
  75.8 167.9 %all-gather.15.cloned.1.call-start = ((), (), s32[]{:S(2)}) async-start(), calls=%async_computation.5 | async-start | bytes 4718592 | tf_op jit(solution)/shard_map/all_gather | solution.py:28
  178.2 3.5 copy-start.1
  178.2 2.0 copy-start
  178.2 2.2 copy-start.9
  190.2 146.2 %all-gather.17.cloned.1.call-start = ((), (), s32[]{:S(2)}) async-start(), calls=%async_computation.6 | async-start | bytes 4718592 | tf_op jit(solution)/shard_map/all_gather | solution.py:28
  269.2 5.4 %collective-permute-start = (bf16[128,4096]{0,1:T(8,128)(2,1)}, bf16[128,4096]{0,1:T(8,128)(2,1)}, u32[]{:S(2)}, u32[]{:S(2)}) collective-permute-start(bf16[128,4096]{0,1:T(8,128)(2,1)} %fusion.14), channel_id=1, source_target_pairs={{1,0},{3,2},{5,4},{7,6},{9,8},{11,10},{13,12},{15,14},{17,16},{19,... | collective-permute-start | bytes 3145736 | tf_op jit(solution)/shard_map/ppermute | solution.py:34
  273.0 3.4 copy-start.10
  274.5 3.6 copy-start.25
  276.5 3.2 copy-start.6
  276.5 3.3 copy-start.28
  278.1 3.4 copy-start.16
  278.1 3.4 copy-start.18
  279.7 1.7 copy-start.12
  279.7 1.9 copy-start.27
  281.7 2.5 copy-start.7
  283.4 114.3 %all-gather.11.cloned.1.call-start = ((), (), s32[]{:S(2)}) async-start(), calls=%async_computation.3 | async-start | bytes 4456448 | tf_op jit(solution)/shard_map/all_gather | solution.py:20
  284.2 2.3 copy-start.13
  286.5 2.6 copy-start.2
  288.1 2.5 copy-start.19
  288.1 2.7 copy-start.17
  292.1 52.6 %all-to-all-start.1 = ((bf16[128,16,256]{2,0,1:T(8,128)(2,1)}), bf16[128,16,256]{2,0,1:T(8,128)(2,1)}, u32[]{:S(2)}, u32[]{:S(2)}) async-start(bf16[128,16,256]{2,0,1:T(8,128)(2,1)} %pad_maximum_fusion.2), calls=%async_computation.1 | async-start | bytes 2097152 | tf_op jit(solution)/shard_map/all_to_all | solution.py:145
  340.4 1.9 copy-start.4
  344.8 56.2 %all-to-all-start = ((bf16[128,16,128]{2,0,1:T(8,128)(2,1)}), bf16[128,16,128]{2,0,1:T(8,128)(2,1)S(1)}, u32[]{:S(2)}, u32[]{:S(2)}) async-start(bf16[128,16,128]{2,0,1:T(8,128)(2,1)} %copy.39), calls=%async_computation | async-start | bytes 1048576 | tf_op jit(solution)/shard_map/all_to_all | solution.py:144
  400.9 48.7 %copy-start.20 = (f32[1,256,512]{2,1,0:T(8,128)S(1)}, f32[1,256,512]{2,1,0:T(8,128)}, u32[]{:S(2)}) copy-start(f32[1,256,512]{2,1,0:T(8,128)} %param.20) | copy-start | bytes 1572868
  400.9 48.8 %copy-start.21 = (f32[1,256,512]{2,1,0:T(8,128)S(1)}, f32[1,256,512]{2,1,0:T(8,128)}, u32[]{:S(2)}) copy-start(f32[1,256,512]{2,1,0:T(8,128)} %param.21) | copy-start | bytes 1572868
  403.7 48.3 %copy-start.22 = (f32[1,128,512]{2,1,0:T(8,128)S(1)}, f32[1,128,512]{2,1,0:T(8,128)}, u32[]{:S(2)}) copy-start(f32[1,128,512]{2,1,0:T(8,128)} %param.18) | copy-start | bytes 786436
  403.7 48.3 %copy-start.23 = (f32[1,128,512]{2,1,0:T(8,128)S(1)}, f32[1,128,512]{2,1,0:T(8,128)}, u32[]{:S(2)}) copy-start(f32[1,128,512]{2,1,0:T(8,128)} %param.19) | copy-start | bytes 786436
  (6 other events, 9.1 us)
Sparse Core Ops, SparseCore 0:
  10.3 40.4 all-gather.8
  75.9 96.6 all-gather.12
  190.3 53.3 all-gather.14
  283.5 52.8 all-gather.16
  339.3 58.3 all-gather.10
